TPU v7x, 32 devices: a whole 2x2x4 slice. The times are simulated.
32 devices in a mesh: space: 8 (over z, y), chan: 2 (over core), filt: 2 (over x).
Axes of the slice: x: 2, y: 2, z: 4, core: 2. Of those that a mesh axis runs over, the one named last changes fastest.
Arguments:
- activation: bfloat16 [8, 512, 512], P('space', ('chan', 'filt')), may hold values from -6 to 6
- kernel: bfloat16 [3, 3, 3, 512, 512], P(None, None, None, 'filt', 'chan'), may hold values from -0.0546875 to 0.0546875
- out_grad: bfloat16 [8, 512, 512], P('space', 'filt', 'chan'), may hold values from -6 to 6
Outputs:
- output: bfloat16 [8, 512, 512], P('space', 'filt', 'chan')
- input_grad: bfloat16 [8, 512, 512], P('space', ('chan', 'filt'))
- kernel_grad: float32 [3, 3, 3, 512, 512], P(None, None, None, 'filt', 'chan')
All inputs are finite; a program needn't handle non-finite values.
Results may differ from a plain program's by a relative error of at most 0.001.
Values may be sent and summed in bfloat16 or wider, within the bound.
A program may use at most 128 MiB of HBM per device.

v0:
```python
import jax
import jax.numpy as jnp
from jax import lax
from jax.sharding import PartitionSpec as P

W = 16


def padded(x, sides, width):
    for axis, dim in sides:
        size, length = (lax.axis_size(axis), x.shape[dim])
        up = [(i, (i + 1) % size) for i in range(size - 1)]
        down = [(j, i) for i, j in up]
        last = lax.slice_in_dim(x, length - width, length, axis=dim)
        first = lax.slice_in_dim(x, 0, width, axis=dim)
        before = lax.ppermute(last, axis, up)
        after = lax.ppermute(first, axis, down)
        x = jnp.concatenate([before, x, after], axis=dim)
    return x


def plane_window(widened, plane, row_step, col_step, masks):
    begin = row_step * W + col_step
    return widened[:, :, begin : begin + plane] * masks[col_step]


def body(activation, kernel, out_grad):
    depth = activation.shape[0]
    plane = activation.shape[2]
    panels = lax.all_gather(activation, "filt", axis=1, tiled=True)
    rimmed = padded(panels, (("space", 0),), 1)
    grad_full = lax.all_gather(out_grad, "chan", axis=2, tiled=True)
    grad_rimmed = padded(grad_full, (("space", 0),), 1)
    column = lax.iota(jnp.int32, plane) % W
    masks = [
        ((column + step - 1 >= 0) & (column + step - 1 < W)).astype(jnp.bfloat16)
        for step in range(3)
    ]
    chan_local = rimmed.shape[1]
    filt_local = grad_rimmed.shape[1]
    wide_input = jnp.pad(rimmed, ((0, 0), (0, 0), (W + 1, W + 1)))
    wide_grad = jnp.pad(grad_rimmed, ((0, 0), (0, 0), (W + 1, W + 1)))
    forward = jnp.zeros((depth, filt_local, plane), jnp.float32)
    backward = jnp.zeros((depth, chan_local, plane), jnp.float32)
    taps = []
    for a in range(3):
        input_slab = wide_input[a : a + depth]
        grad_slab = wide_grad[2 - a : 2 - a + depth]
        for b in range(3):
            window = jnp.concatenate(
                [plane_window(input_slab, plane, b, c, masks) for c in range(3)], axis=1
            )
            grad_window = jnp.concatenate(
                [plane_window(grad_slab, plane, 2 - b, 2 - c, masks) for c in range(3)], axis=1
            )
            weights = kernel[a, b]
            forward_weights = weights.transpose(1, 0, 2).reshape(filt_local, 3 * chan_local)
            backward_weights = weights.reshape(3 * filt_local, chan_local)
            forward = forward + jnp.einsum(
                "fk,zkp->zfp", forward_weights, window, preferred_element_type=jnp.float32
            )
            backward = backward + jnp.einsum(
                "fk,zfp->zkp", backward_weights, grad_window, preferred_element_type=jnp.float32
            )
            joined = jnp.einsum(
                "zfp,zkp->fk", grad_full, window, preferred_element_type=jnp.float32
            )
            taps.append(joined.reshape(filt_local, 3, chan_local).transpose(1, 0, 2))
    output = lax.psum_scatter(forward, "chan", scatter_dimension=2, tiled=True).astype(jnp.bfloat16)
    input_grad = lax.psum_scatter(backward, "filt", scatter_dimension=1, tiled=True).astype(
        jnp.bfloat16
    )
    local_grad = jnp.stack(taps).reshape(3, 3, 3, filt_local, chan_local)
    total = lax.psum(local_grad, "space")
    cells = depth * lax.axis_size("space") * plane
    kernel_grad = total / jnp.sqrt(jnp.float32(cells))
    return (output, input_grad, kernel_grad)


def solution(mesh):
    placed = (
        P("space", ("chan", "filt"), None),
        P(None, None, None, "filt", "chan"),
        P("space", "filt", "chan"),
    )
    return jax.shard_map(
        body,
        mesh=mesh,
        in_specs=placed,
        out_specs=(
            P("space", "filt", "chan"),
            P("space", ("chan", "filt"), None),
            P(None, None, None, "filt", "chan"),
        ),
        check_vma=False,
    )
```

profile of v0, /device:TPU:0, one launch (start us, length us, event | category | flops | bytes accessed | tf_op | source)
XLA Modules:
  0.0 349.9 jit_solution(17022431209506651574)
XLA Ops:
  8.0 7.4 %all_gather.6 = bf16[1,256,512]{2,1,0:T(8,128)(2,1)S(1)} all-gather(bf16[1,128,512]{2,1,0:T(8,128)(2,1)} %param.3), channel_id=1, replica_groups=mesh['space'=8,'chan'=2,'filt'=2] {'filt'}, dimensions={1}, use_global_device_ids=true | all-gather | bytes 393216 | tf_op jit(solution)/shard_map/all_gather | solution.py:30
  15.4 1.3 collective-permute-start.1
  16.7 5.3 %collective-permute-start = (bf16[1,256,512]{2,1,0:T(8,128)(2,1)S(1)}, bf16[1,256,512]{2,1,0:T(8,128)(2,1)}, u32[]{:S(2)}, u32[]{:S(2)}) collective-permute-start(bf16[1,256,512]{2,1,0:T(8,128)(2,1)S(1)} %all_gather.6), channel_id=1, source_target_pairs={{0,4},{4,8},{8,12},{12,16},{16,20},{20,24},{24,28},{1,5},{5,9},{9,... | collective-permute-start | bytes 786440 | tf_op jit(solution)/shard_map/ppermute | solution.py:16
  22.0 2.3 all_gather.7
  24.2 4.5 %collective-permute-start.2 = (bf16[1,256,512]{2,1,0:T(8,128)(2,1)S(1)}, bf16[1,256,512]{2,1,0:T(8,128)(2,1)}, u32[]{:S(2)}, u32[]{:S(2)}) collective-permute-start(bf16[1,256,512]{2,1,0:T(8,128)(2,1)S(1)} %all_gather.7), channel_id=1, source_target_pairs={{0,4},{4,8},{8,12},{12,16},{16,20},{20,24},{24,28},{1,5},{5,9},{9,... | collective-permute-start | bytes 786440 | tf_op jit(solution)/shard_map/ppermute | solution.py:16
  28.8 1.3 collective-permute-start.3
  30.1 3.2 fusion.87
  33.3 2.3 copy.42
  35.6 1.9 copy.43
  37.5 0.9 copy.44
  38.5 0.9 copy.45
  39.4 0.9 copy.46
  40.3 0.9 copy.47
  41.2 0.9 copy.48
  42.2 1.0 copy.49
  43.1 0.9 copy.50
  44.1 1.5 select_maximum_fusion.2
  45.6 0.7 slice_multiply_fusion.24
  46.3 1.6 select_maximum_fusion
  48.0 1.9 slice_multiply_fusion
  49.8 2.8 slice_multiply_fusion.26
  53.0 4.0 %slice_multiply_fusion.2 = (bf16[1,256,512]{2,1,0:T(8,128)(2,1)}, bf16[1,256,512]{2,1,0:T(8,128)(2,1)}, bf16[1,256,512]{2,1,0:T(8,128)(2,1)}, bf16[1,256,512]{2,...) fusion(bf16[3,256,546]{2,1,0:T(8,128)(2,1)S(1)} %select_maximum, ...), kind=kLoop, calls=%fused_computation.112 | loop fusion | flops 2228224 | bytes 8914944 | tf_op jit(solution)/shard_map/mul | solution.py:24
  57.1 0.9 copy-done.34
  58.4 0.6 copy-done.33
  59.4 1.1 pad_maximum_fusion.2
  61.9 1.2 pad_maximum_fusion.4
  64.6 1.8 broadcast_multiply_fusion.3
  66.4 1.3 pad_maximum_fusion.6
  68.6 1.2 fusion.10
  70.1 1.6 fusion.13
  77.9 0.9 copy-done.10
  81.5 1.2 fusion.11
  82.8 1.3 fusion.9
  84.1 1.3 fusion.8
  85.4 1.3 fusion.7
  86.7 1.3 fusion.6
  88.0 1.3 fusion.5
  89.3 1.3 fusion.4
  90.5 1.3 fusion.3
  91.8 1.3 fusion.2
  93.1 1.3 fusion.1
  94.4 8.1 %copy.39 = f32[3,3,3,256,256]{4,3,2,1,0:T(8,128)} copy(f32[3,3,3,256,256]{3,4,2,1,0:T(8,128)} %bitcast.227) | data formatting | bytes 14155776 | tf_op jit(solution)/shard_map/reshape | solution.py:73
  102.5 1.0 convert_element_type.135
  103.5 0.8 copy.40
  104.3 1.0 convert_element_type.136
  105.2 0.8 copy.41
  106.0 229.8 %all-reduce.4.cloned.1.call-done = f32[3,3,3,256,256]{4,3,2,1,0:T(8,128)} async-done(((f32[3,3,3,256,256]{4,3,2,1,0:T(8,128)}), f32[3,3,3,256,256]{4,3,2,1,0:T(8,128)}) %all-reduce.4.cloned.1.call-update) | async-done | bytes 7077904 | tf_op jit(solution)/shard_map/psum | solution.py:74
  335.8 6.7 %broadcast_multiply_fusion = f32[3,3,3,256,256]{4,3,2,1,0:T(8,128)} fusion(f32[3,3,3,256,256]{4,3,2,1,0:T(8,128)} %all-reduce.4.cloned.1.call-done), kind=kLoop, calls=%fused_computation | loop fusion | flops 1769472 | bytes 14155776 | tf_op jit(solution)/shard_map/div | solution.py:76
  (149 shorter events, 14.3 us)
Async XLA Ops:
  8.0 94.5 %reduce-scatter.3.cloned.1.call-start = ((), (), s32[]{:S(2)}) async-start(), calls=%async_computation.2 | async-start | bytes 786432 | tf_op jit(solution)/shard_map/reduce_scatter | solution.py:69
  15.4 28.7 %collective-permute-start.1 = (bf16[1,256,512]{2,1,0:T(8,128)(2,1)S(1)}, bf16[1,256,512]{2,1,0:T(8,128)(2,1)}, u32[]{:S(2)}, u32[]{:S(2)}) collective-permute-start(bf16[1,256,512]{2,1,0:T(8,128)(2,1)S(1)} %all_gather.6), channel_id=1, source_target_pairs={{4,0},{8,4},{12,8},{16,12},{20,16},{24,20},{28,24},{5,1},{9,5},{13... | collective-permute-start | bytes 786440 | tf_op jit(solution)/shard_map/ppermute | solution.py:17
  16.7 27.4 %collective-permute-start = (bf16[1,256,512]{2,1,0:T(8,128)(2,1)S(1)}, bf16[1,256,512]{2,1,0:T(8,128)(2,1)}, u32[]{:S(2)}, u32[]{:S(2)}) collective-permute-start(bf16[1,256,512]{2,1,0:T(8,128)(2,1)S(1)} %all_gather.6), channel_id=1, source_target_pairs={{0,4},{4,8},{8,12},{12,16},{16,20},{20,24},{24,28},{1,5},{5,9},{9,... | collective-permute-start | bytes 786440 | tf_op jit(solution)/shard_map/ppermute | solution.py:16
  24.2 22.1 %collective-permute-start.2 = (bf16[1,256,512]{2,1,0:T(8,128)(2,1)S(1)}, bf16[1,256,512]{2,1,0:T(8,128)(2,1)}, u32[]{:S(2)}, u32[]{:S(2)}) collective-permute-start(bf16[1,256,512]{2,1,0:T(8,128)(2,1)S(1)} %all_gather.7), channel_id=1, source_target_pairs={{0,4},{4,8},{8,12},{12,16},{16,20},{20,24},{24,28},{1,5},{5,9},{9,... | collective-permute-start | bytes 786440 | tf_op jit(solution)/shard_map/ppermute | solution.py:16
  28.8 17.6 %collective-permute-start.3 = (bf16[1,256,512]{2,1,0:T(8,128)(2,1)S(1)}, bf16[1,256,512]{2,1,0:T(8,128)(2,1)}, u32[]{:S(2)}, u32[]{:S(2)}) collective-permute-start(bf16[1,256,512]{2,1,0:T(8,128)(2,1)S(1)} %all_gather.7), channel_id=1, source_target_pairs={{4,0},{8,4},{12,8},{16,12},{20,16},{24,20},{28,24},{5,1},{9,5},{13... | collective-permute-start | bytes 786440 | tf_op jit(solution)/shard_map/ppermute | solution.py:17
  33.3 6.1 %copy-start.15 = (bf16[1,1,3,256,256]{4,3,2,1,0:T(8,128)(2,1)}, bf16[1,1,3,256,256]{4,3,2,1,0:T(8,128)(2,1)S(1)}, u32[]{:S(2)}) copy-start(bf16[1,1,3,256,256]{4,3,2,1,0:T(8,128)(2,1)S(1)} %get-tuple-element.17) | copy-start | bytes 1179652
  33.3 6.1 %copy-start.17 = (bf16[1,1,3,256,256]{4,3,2,1,0:T(8,128)(2,1)}, bf16[1,1,3,256,256]{4,3,2,1,0:T(8,128)(2,1)S(1)}, u32[]{:S(2)}) copy-start(bf16[1,1,3,256,256]{4,3,2,1,0:T(8,128)(2,1)S(1)} %get-tuple-element.18) | copy-start | bytes 1179652
  33.3 6.1 %copy-start.13 = (bf16[1,1,3,256,256]{4,3,2,1,0:T(8,128)(2,1)}, bf16[1,1,3,256,256]{4,3,2,1,0:T(8,128)(2,1)S(1)}, u32[]{:S(2)}) copy-start(bf16[1,1,3,256,256]{4,3,2,1,0:T(8,128)(2,1)S(1)} %get-tuple-element.16) | copy-start | bytes 1179652
  33.3 7.0 %copy-start.11 = (bf16[1,1,3,256,256]{4,3,2,1,0:T(8,128)(2,1)}, bf16[1,1,3,256,256]{4,3,2,1,0:T(8,128)(2,1)S(1)}, u32[]{:S(2)}) copy-start(bf16[1,1,3,256,256]{4,3,2,1,0:T(8,128)(2,1)S(1)} %get-tuple-element.15) | copy-start | bytes 1179652
  33.3 7.9 %copy-start.9 = (bf16[1,1,3,256,256]{4,3,2,1,0:T(8,128)(2,1)}, bf16[1,1,3,256,256]{4,3,2,1,0:T(8,128)(2,1)S(1)}, u32[]{:S(2)}) copy-start(bf16[1,1,3,256,256]{4,3,2,1,0:T(8,128)(2,1)S(1)} %get-tuple-element.14) | copy-start | bytes 1179652
  33.3 8.8 %copy-start.7 = (bf16[1,1,3,256,256]{4,3,2,1,0:T(8,128)(2,1)}, bf16[1,1,3,256,256]{4,3,2,1,0:T(8,128)(2,1)S(1)}, u32[]{:S(2)}) copy-start(bf16[1,1,3,256,256]{4,3,2,1,0:T(8,128)(2,1)S(1)} %get-tuple-element.13) | copy-start | bytes 1179652
  33.3 9.8 %copy-start.5 = (bf16[1,1,3,256,256]{4,3,2,1,0:T(8,128)(2,1)}, bf16[1,1,3,256,256]{4,3,2,1,0:T(8,128)(2,1)S(1)}, u32[]{:S(2)}) copy-start(bf16[1,1,3,256,256]{4,3,2,1,0:T(8,128)(2,1)S(1)} %get-tuple-element.12) | copy-start | bytes 1179652
  46.3 21.7 %copy-start.21 = (bf16[1,256,512]{2,1,0:T(8,128)(2,1)}, bf16[1,256,512]{2,1,0:T(8,128)(2,1)S(1)}, u32[]{:S(2)}) copy-start(bf16[1,256,512]{2,1,0:T(8,128)(2,1)S(1)} %get-tuple-element.60) | copy-start | bytes 786436
  49.8 2.8 copy-start.35
  52.6 15.5 %copy-start.23 = (bf16[1,256,512]{2,1,0:T(8,128)(2,1)}, bf16[1,256,512]{2,1,0:T(8,128)(2,1)S(1)}, u32[]{:S(2)}) copy-start(bf16[1,256,512]{2,1,0:T(8,128)(2,1)S(1)} %get-tuple-element.45) | copy-start | bytes 786436
  52.6 15.5 %copy-start.25 = (bf16[1,256,512]{2,1,0:T(8,128)(2,1)}, bf16[1,256,512]{2,1,0:T(8,128)(2,1)S(1)}, u32[]{:S(2)}) copy-start(bf16[1,256,512]{2,1,0:T(8,128)(2,1)S(1)} %get-tuple-element.80) | copy-start | bytes 786436
  61.9 1.3 copy-start.30
  66.4 1.3 copy-start.28
  68.6 1.5 copy-start.20
  69.9 34.4 %reduce-scatter.5.cloned.1.call-start = ((), (), s32[]{:S(2)}) async-start(), calls=%async_computation.3 | async-start | bytes 786432 | tf_op jit(solution)/shard_map/reduce_scatter | solution.py:70
  70.1 1.7 copy-start.19
  70.1 1.7 copy-start.46
  70.1 1.7 copy-start.58
  70.1 1.7 copy-start.59
  71.8 1.1 copy-start.56
  71.8 1.2 copy-start.57
  73.0 1.1 copy-start.54
  73.0 1.2 copy-start.55
  74.3 1.1 copy-start.41
  74.3 1.1 copy-start.47
  74.3 1.2 copy-start.53
  75.5 1.1 copy-start.51
  75.5 1.2 copy-start.52
  76.7 1.1 copy-start.26
  77.8 1.1 copy-start.38
  77.8 1.2 copy-start.49
  77.8 1.2 copy-start.50
  79.1 1.1 copy-start.37
  79.1 1.2 copy-start.40
  79.1 1.2 copy-start.48
  80.3 1.1 copy-start.44
  80.3 1.2 copy-start.45
  84.0 1.4 copy-start
  84.1 251.7 %all-reduce.4.cloned.1.call-start = ((), (), s32[]{:S(2)}) async-start(), calls=%async_computation.4 | async-start | bytes 14155776 | tf_op jit(solution)/shard_map/psum | solution.py:74
  85.4 2.6 copy-start.2
  86.7 2.6 copy-start.1
  88.0 2.6 copy-start.4
  89.3 2.6 copy-start.3
  (19 other events, 19.3 us)
Sparse Core Ops, SparseCore 0:
  70.0 9.3 reduce-scatter.2
  84.2 16.0 reduce-scatter.4
Sparse Core Ops, SparseCore 1:
  102.6 233.1 all-reduce.3
where the time goes:
time: 351 us; the launch traced here: 350 us
  waiting for transfers between devices  230 us (66%)
  local copies, waits for them, and re-layouts  33.5 us (10%)
  other arithmetic  26.6 us (8%)
  matrix products  21.7 us (6%)
  between operations  16 us (5%)
  starting transfers between devices  12.7 us (4%)
  blocking collectives  9.65 us (3%)
    psum x1, waiting for transfers between devices, body(): total = lax.psum(local_grad, 'space')  230 us
    unnamed x131, local copies, waits for them, and re-layouts  22.2 us
    dot_general x9, matrix products, body(): jnp.einsum('zfp,zkp->fk', grad_full, window, preferred_element_type=jnp.f...  11.5 us
    mul x5, other arithmetic, plane_window(): return widened[:, :, begin:begin + plane] * masks[col_step]  11.1 us
    ppermute x2, starting transfers between devices, padded(): before = lax.ppermute(last, axis, up)  9.8 us
    reshape x1, local copies, waits for them, and re-layouts, body(): local_grad = jnp.stack(taps).reshape(3, 3, 3, filt_local, chan_local)  8.09 us
    all_gather x1, blocking collectives, body(): panels = lax.all_gather(activation, 'filt', axis=1, tiled=True)  7.36 us
  transfers between devices with their start and end apart: 7, of which 1 were waited for; matrix products, arithmetic and copies ran while one was open for 13% of the time, Pallas kernels for 0%

commit v1 on v0

--- a/solution.py
+++ b/solution.py
@@ -4,6 +4,15 @@
 from jax.sharding import PartitionSpec as P
 
 W = 16
+
+
+def add_in_pairs(x, mesh_axis):
+    count = lax.axis_size(mesh_axis)
+    acc, stride = (x, 1)
+    while stride < count:
+        acc = acc + lax.ppermute(acc, mesh_axis, [(i, i ^ stride) for i in range(count)])
+        stride = 2 * stride
+    return acc
 
 
 def padded(x, sides, width):
@@ -71,7 +80,7 @@
         jnp.bfloat16
     )
     local_grad = jnp.stack(taps).reshape(3, 3, 3, filt_local, chan_local)
-    total = lax.psum(local_grad, "space")
+    total = add_in_pairs(local_grad, "space")
     cells = depth * lax.axis_size("space") * plane
     kernel_grad = total / jnp.sqrt(jnp.float32(cells))
     return (output, input_grad, kernel_grad)

time: 351 us -> 708 us (2.02)
  waiting for transfers between devices: 230 us -> 580 us
  matrix products: 21.7 us -> 13.9 us
    ppermute x0 -> x3, waiting for transfers between devices: none -> 557 us  [add_in_pairs(): lax.ppermute(acc, mesh_axis, [(i, i ^ stride) for i in range(count)])]
    psum x1 -> x0, waiting for transfers between devices: 230 us -> none  [body(): total = lax.psum(local_grad, 'space')]
    add x0 -> x2, other arithmetic: none -> 13.1 us  [add_in_pairs(): acc + lax.ppermute(acc, mesh_axis, [(i, i ^ stride) for i in range(count)])]
    reduce_scatter x1, waiting for transfers between devices: 0.01 us -> 12.1 us  [body(): lax.psum_scatter(backward, 'filt', scatter_dimension=1, tiled=True)]
    ppermute x2, waiting for transfers between devices: 0.01 us -> 10.7 us  [padded(): before = lax.ppermute(last, axis, up)]
    dot_general x9, matrix products: 11.5 us -> 3.57 us  [body(): jnp.einsum('zfp,zkp->fk', grad_full, window, preferred_element_type=jnp.f...]
    unnamed x131 -> x175, local copies, waits for them, and re-layouts: 22.2 us -> 28.5 us
  transfers between devices with their start and end apart: 7 -> 9, of which waited for: 1 -> 6; matrix products, arithmetic and copies ran while one was open for 13% -> 4% of each run, Pallas kernels for 0% -> 0%
where the time goes in v1:
time: 708 us; the launch traced here: 707 us
  waiting for transfers between devices  580 us (82%)
  local copies, waits for them, and re-layouts  37.8 us (5%)
  other arithmetic  32.4 us (5%)
  starting transfers between devices  18.6 us (3%)
  between operations  14.9 us (2%)
  matrix products  13.9 us (2%)
  blocking collectives  9.66 us (1%)
    ppermute x3, waiting for transfers between devices, add_in_pairs(): lax.ppermute(acc, mesh_axis, [(i, i ^ stride) for i in range(count)])  557 us
    unnamed x175, local copies, waits for them, and re-layouts  28.5 us
  transfers between devices with their start and end apart: 9, of which 6 were waited for; matrix products, arithmetic and copies ran while one was open for 4% of the time, Pallas kernels for 0%

profile of v1, /device:TPU:0, one launch (start us, length us, event | category | flops | bytes accessed | tf_op | source)
XLA Modules:
  0.0 707.5 jit_solution(4448855264208471827)
XLA Ops:
  7.2 7.4 %all_gather.6 = bf16[1,256,512]{2,1,0:T(8,128)(2,1)S(1)} all-gather(bf16[1,128,512]{2,1,0:T(8,128)(2,1)} %param.3), channel_id=1, replica_groups=mesh['space'=8,'chan'=2,'filt'=2] {'filt'}, dimensions={1}, use_global_device_ids=true | all-gather | bytes 393216 | tf_op jit(solution)/shard_map/all_gather | solution.py:39
  14.6 1.3 collective-permute-start.1
  15.9 4.6 collective-permute-start
  20.4 2.3 all_gather.7
  22.7 4.5 collective-permute-start.2
  27.3 1.3 collective-permute-start.3
  28.6 0.9 collective-permute-done
  30.0 0.7 slice_multiply_fusion.24
  30.8 9.8 %collective-permute-done.2 = bf16[1,256,512]{2,1,0:T(8,128)(2,1)S(1)} collective-permute-done((bf16[1,256,512]{2,1,0:T(8,128)(2,1)S(1)}, bf16[1,256,512]{2,1,0:T(8,128)(2,1)S(1)}, u32[]{:S(2)}, u32[]{:S(2)}) %collective-permute-start.2) | collective-permute-done | bytes 262176 | tf_op jit(solution)/shard_map/ppermute | solution.py:25
  41.2 1.7 slice_multiply_fusion.26
  43.0 3.0 slice_multiply_fusion.2
  46.1 0.5 copy-done.46
  49.5 0.7 broadcast_multiply_fusion.2
  50.3 0.6 copy-done.48
  52.2 3.0 copy-done
  55.2 8.1 %copy.42 = f32[3,3,3,256,256]{4,3,2,1,0:T(8,128)} copy(f32[3,3,3,256,256]{3,4,2,1,0:T(8,128)} %bitcast.227) | data formatting | bytes 14155776 | tf_op jit(solution)/shard_map/reshape | solution.py:82
  63.3 2.5 collective-permute-start.4
  65.7 152.9 %collective-permute-done.4 = f32[3,3,3,256,256]{4,3,2,1,0:T(8,128)} collective-permute-done((f32[3,3,3,256,256]{4,3,2,1,0:T(8,128)}, f32[3,3,3,256,256]{4,3,2,1,0:T(8,128)}, u32[]{:S(2)}, u32[]{:S(2)}) %collective-permute-start.4) | collective-permute-done | bytes 7077920 | tf_op jit(solution)/shard_map/ppermute | solution.py:13
  218.6 6.0 add.255
  224.7 1.6 collective-permute-start.5
  226.3 152.3 %collective-permute-done.5 = f32[3,3,3,256,256]{4,3,2,1,0:T(8,128)} collective-permute-done((f32[3,3,3,256,256]{4,3,2,1,0:T(8,128)S(1)}, f32[3,3,3,256,256]{4,3,2,1,0:T(8,128)}, u32[]{:S(2)}, u32[]{:S(2)}) %collective-permute-start.5) | collective-permute-done | bytes 7077920 | tf_op jit(solution)/shard_map/ppermute | solution.py:13
  378.6 7.1 add.256
  385.7 2.6 collective-permute-start.6
  388.2 1.2 fusion.87
  389.4 1.9 copy.45
  391.4 1.9 copy.46
  393.3 1.9 copy.47
  395.2 0.9 copy.48
  396.2 0.9 copy.49
  397.1 0.9 copy.50
  398.0 0.9 copy.51
  398.9 0.9 copy.52
  399.9 1.0 copy.53
  400.8 1.7 fusion.58
  411.3 1.3 fusion.10
  414.4 0.6 copy-done.3
  415.5 0.6 copy-done.2
  417.7 0.5 copy-done.68
  418.7 0.5 copy-done.71
  419.8 0.5 copy-done.69
  422.4 1.2 fusion.11
  423.7 1.0 convert_element_type.135
  424.7 0.8 copy.43
  425.5 12.1 %reduce-scatter.5.cloned.1.call-done = f32[1,128,512]{1,2,0:T(8,128)} async-done(((f32[1,256,512]{1,2,0:T(8,128)}), f32[1,128,512]{1,2,0:T(8,128)}) %reduce-scatter.5.cloned.1.call-update) | async-done | bytes 262160 | tf_op jit(solution)/shard_map/reduce_scatter | solution.py:79
  437.6 1.0 convert_element_type.136
  438.5 0.8 copy.44
  439.3 252.1 %collective-permute-done.6 = f32[3,3,3,256,256]{4,3,2,1,0:T(8,128)} collective-permute-done((f32[3,3,3,256,256]{4,3,2,1,0:T(8,128)}, f32[3,3,3,256,256]{4,3,2,1,0:T(8,128)}, u32[]{:S(2)}, u32[]{:S(2)}) %collective-permute-start.6) | collective-permute-done | bytes 7077920 | tf_op jit(solution)/shard_map/ppermute | solution.py:13
  691.4 9.2 %add_multiply_fusion = f32[3,3,3,256,256]{4,3,2,1,0:T(8,128)} fusion(f32[3,3,3,256,256]{4,3,2,1,0:T(8,128)} %add.256, f32[3,3,3,256,256]{4,3,2,1,0:T(8,128)} %collective-permute-done.6), kind=kLoop, calls=%fused_computation | loop fusion | flops 3538944 | bytes 21233664 | tf_op jit(solution)/shard_map/div | solution.py:85
  (198 shorter events, 20.9 us)
Async XLA Ops:
  7.2 416.5 %reduce-scatter.3.cloned.1.call-start = ((), (), s32[]{:S(2)}) async-start(), calls=%async_computation.2 | async-start | bytes 786432 | tf_op jit(solution)/shard_map/reduce_scatter | solution.py:78
  14.6 14.0 %collective-permute-start.1 = (bf16[1,256,512]{2,1,0:T(8,128)(2,1)S(1)}, bf16[1,256,512]{2,1,0:T(8,128)(2,1)S(1)}, u32[]{:S(2)}, u32[]{:S(2)}) collective-permute-start(bf16[1,256,512]{2,1,0:T(8,128)(2,1)S(1)} %all_gather.6), channel_id=1, source_target_pairs={{4,0},{8,4},{12,8},{16,12},{20,16},{24,20},{28,24},{5,1},{9,5},{13... | collective-permute-start | bytes 786440 | tf_op jit(solution)/shard_map/ppermute | solution.py:26
  15.9 13.6 %collective-permute-start = (bf16[1,256,512]{2,1,0:T(8,128)(2,1)S(1)}, bf16[1,256,512]{2,1,0:T(8,128)(2,1)S(1)}, u32[]{:S(2)}, u32[]{:S(2)}) collective-permute-start(bf16[1,256,512]{2,1,0:T(8,128)(2,1)S(1)} %all_gather.6), channel_id=1, source_target_pairs={{0,4},{4,8},{8,12},{12,16},{16,20},{20,24},{24,28},{1,5},{5,9},{9,... | collective-permute-start | bytes 786440 | tf_op jit(solution)/shard_map/ppermute | solution.py:25
  22.7 17.9 %collective-permute-start.2 = (bf16[1,256,512]{2,1,0:T(8,128)(2,1)S(1)}, bf16[1,256,512]{2,1,0:T(8,128)(2,1)S(1)}, u32[]{:S(2)}, u32[]{:S(2)}) collective-permute-start(bf16[1,256,512]{2,1,0:T(8,128)(2,1)S(1)} %all_gather.7), channel_id=1, source_target_pairs={{0,4},{4,8},{8,12},{12,16},{16,20},{20,24},{24,28},{1,5},{5,9},{9,... | collective-permute-start | bytes 786440 | tf_op jit(solution)/shard_map/ppermute | solution.py:25
  27.3 13.4 %collective-permute-start.3 = (bf16[1,256,512]{2,1,0:T(8,128)(2,1)S(1)}, bf16[1,256,512]{2,1,0:T(8,128)(2,1)S(1)}, u32[]{:S(2)}, u32[]{:S(2)}) collective-permute-start(bf16[1,256,512]{2,1,0:T(8,128)(2,1)S(1)} %all_gather.7), channel_id=1, source_target_pairs={{4,0},{8,4},{12,8},{16,12},{20,16},{24,20},{28,24},{5,1},{9,5},{13... | collective-permute-start | bytes 786440 | tf_op jit(solution)/shard_map/ppermute | solution.py:26
  30.7 15.3 %copy-start.27 = (bf16[1,256,512]{2,1,0:T(8,128)(2,1)}, bf16[1,256,512]{2,1,0:T(8,128)(2,1)S(1)}, u32[]{:S(2)}) copy-start(bf16[1,256,512]{2,1,0:T(8,128)(2,1)S(1)} %get-tuple-element.67) | copy-start | bytes 786436
  30.7 15.3 %copy-start.31 = (bf16[1,256,512]{2,1,0:T(8,128)(2,1)}, bf16[1,256,512]{2,1,0:T(8,128)(2,1)S(1)}, u32[]{:S(2)}) copy-start(bf16[1,256,512]{2,1,0:T(8,128)(2,1)S(1)} %get-tuple-element.68) | copy-start | bytes 786436
  30.7 16.8 %copy-start.13 = (bf16[1,256,512]{2,1,0:T(8,128)(2,1)}, bf16[1,256,512]{2,1,0:T(8,128)(2,1)S(1)}, u32[]{:S(2)}) copy-start(bf16[1,256,512]{2,1,0:T(8,128)(2,1)S(1)} %get-tuple-element.65) | copy-start | bytes 786436
  30.7 16.8 %copy-start.21 = (bf16[1,256,512]{2,1,0:T(8,128)(2,1)}, bf16[1,256,512]{2,1,0:T(8,128)(2,1)S(1)}, u32[]{:S(2)}) copy-start(bf16[1,256,512]{2,1,0:T(8,128)(2,1)S(1)} %get-tuple-element.66) | copy-start | bytes 786436
  30.7 17.8 %copy-start.9 = (bf16[1,256,512]{2,1,0:T(8,128)(2,1)}, bf16[1,256,512]{2,1,0:T(8,128)(2,1)S(1)}, u32[]{:S(2)}) copy-start(bf16[1,256,512]{2,1,0:T(8,128)(2,1)S(1)} %get-tuple-element.63) | copy-start | bytes 786436
  30.7 17.8 %copy-start.11 = (bf16[1,256,512]{2,1,0:T(8,128)(2,1)}, bf16[1,256,512]{2,1,0:T(8,128)(2,1)S(1)}, u32[]{:S(2)}) copy-start(bf16[1,256,512]{2,1,0:T(8,128)(2,1)S(1)} %get-tuple-element.64) | copy-start | bytes 786436
  30.8 19.5 %copy-start.5 = (bf16[1,256,512]{2,1,0:T(8,128)(2,1)}, bf16[1,256,512]{2,1,0:T(8,128)(2,1)S(1)}, u32[]{:S(2)}) copy-start(bf16[1,256,512]{2,1,0:T(8,128)(2,1)S(1)} %get-tuple-element.61) | copy-start | bytes 786436
  30.8 19.4 %copy-start.7 = (bf16[1,256,512]{2,1,0:T(8,128)(2,1)}, bf16[1,256,512]{2,1,0:T(8,128)(2,1)S(1)}, u32[]{:S(2)}) copy-start(bf16[1,256,512]{2,1,0:T(8,128)(2,1)S(1)} %get-tuple-element.62) | copy-start | bytes 786436
  30.8 20.9 %copy-start.50 = (bf16[1,256,512]{2,1,0:T(8,128)(2,1)}, bf16[1,256,512]{2,1,0:T(8,128)(2,1)S(1)}, u32[]{:S(2)}) copy-start(bf16[1,256,512]{2,1,0:T(8,128)(2,1)S(1)} %get-tuple-element.60) | copy-start | bytes 786436
  42.9 3.1 copy-start.40
  42.9 3.1 copy-start.44
  42.9 3.1 copy-start.45
  42.9 4.6 copy-start.32
  42.9 4.6 copy-start.34
  42.9 4.6 copy-start.36
  42.9 4.6 copy-start.38
  42.9 5.6 copy-start.23
  42.9 5.6 copy-start.25
  42.9 5.6 copy-start.29
  43.0 7.3 %copy-start.15 = (bf16[1,256,512]{2,1,0:T(8,128)(2,1)}, bf16[1,256,512]{2,1,0:T(8,128)(2,1)S(1)}, u32[]{:S(2)}) copy-start(bf16[1,256,512]{2,1,0:T(8,128)(2,1)S(1)} %get-tuple-element.46) | copy-start | bytes 786436
  43.0 7.3 %copy-start.17 = (bf16[1,256,512]{2,1,0:T(8,128)(2,1)}, bf16[1,256,512]{2,1,0:T(8,128)(2,1)S(1)}, u32[]{:S(2)}) copy-start(bf16[1,256,512]{2,1,0:T(8,128)(2,1)S(1)} %get-tuple-element.47) | copy-start | bytes 786436
  43.0 7.3 %copy-start.19 = (bf16[1,256,512]{2,1,0:T(8,128)(2,1)}, bf16[1,256,512]{2,1,0:T(8,128)(2,1)S(1)}, u32[]{:S(2)}) copy-start(bf16[1,256,512]{2,1,0:T(8,128)(2,1)S(1)} %get-tuple-element.79) | copy-start | bytes 786436
  43.0 8.7 %copy-start.52 = (bf16[1,256,512]{2,1,0:T(8,128)(2,1)}, bf16[1,256,512]{2,1,0:T(8,128)(2,1)S(1)}, u32[]{:S(2)}) copy-start(bf16[1,256,512]{2,1,0:T(8,128)(2,1)S(1)} %get-tuple-element.45) | copy-start | bytes 786436
  43.0 8.7 %copy-start.54 = (bf16[1,256,512]{2,1,0:T(8,128)(2,1)}, bf16[1,256,512]{2,1,0:T(8,128)(2,1)S(1)}, u32[]{:S(2)}) copy-start(bf16[1,256,512]{2,1,0:T(8,128)(2,1)S(1)} %get-tuple-element.80) | copy-start | bytes 786436
  46.0 2.6 copy-start.42
  52.2 3.0 copy-start
  63.3 155.3 %collective-permute-start.4 = (f32[3,3,3,256,256]{4,3,2,1,0:T(8,128)}, f32[3,3,3,256,256]{4,3,2,1,0:T(8,128)}, u32[]{:S(2)}, u32[]{:S(2)}) collective-permute-start(f32[3,3,3,256,256]{4,3,2,1,0:T(8,128)} %copy.42), channel_id=1, source_target_pairs={{0,4},{4,0},{8,12},{12,8},{16,20},{20,16},{24,28},{28,24},{1,5},{5... | collective-permute-start | bytes 21233672 | tf_op jit(solution)/shard_map/ppermute | solution.py:13
  224.7 154.0 %collective-permute-start.5 = (f32[3,3,3,256,256]{4,3,2,1,0:T(8,128)S(1)}, f32[3,3,3,256,256]{4,3,2,1,0:T(8,128)}, u32[]{:S(2)}, u32[]{:S(2)}) collective-permute-start(f32[3,3,3,256,256]{4,3,2,1,0:T(8,128)S(1)} %add.255), channel_id=1, source_target_pairs={{0,8},{4,12},{8,0},{12,4},{16,24},{20,28},{24,16},{28,20},{1,9},{5... | collective-permute-start | bytes 21233672 | tf_op jit(solution)/shard_map/ppermute | solution.py:13
  378.6 9.6 %copy-start.1 = (bf16[3,3,3,256,256]{4,3,2,1,0:T(8,128)(2,1)S(1)}, bf16[3,3,3,256,256]{4,3,2,1,0:T(8,128)(2,1)}, u32[]{:S(2)}) copy-start(bf16[3,3,3,256,256]{4,3,2,1,0:T(8,128)(2,1)} %param.4) | copy-start | bytes 10616836
  385.7 305.8 %collective-permute-start.6 = (f32[3,3,3,256,256]{4,3,2,1,0:T(8,128)}, f32[3,3,3,256,256]{4,3,2,1,0:T(8,128)}, u32[]{:S(2)}, u32[]{:S(2)}) collective-permute-start(f32[3,3,3,256,256]{4,3,2,1,0:T(8,128)} %add.256), channel_id=1, source_target_pairs={{0,16},{4,20},{8,24},{12,28},{16,0},{20,4},{24,8},{28,12},{1,17},{... | collective-permute-start | bytes 21233672 | tf_op jit(solution)/shard_map/ppermute | solution.py:13
  400.8 1.8 copy-start.28
  400.8 1.8 copy-start.41
  400.8 1.8 copy-start.47
  400.8 1.8 copy-start.63
  402.6 1.2 copy-start.62
  403.9 1.2 copy-start.61
  405.1 1.2 copy-start.60
  406.3 1.2 copy-start.59
  407.6 1.2 copy-start.58
  408.8 1.2 copy-start.57
  410.0 1.2 copy-start.56
  412.5 25.0 %reduce-scatter.5.cloned.1.call-start = ((), (), s32[]{:S(2)}) async-start(), calls=%async_computation.3 | async-start | bytes 786432 | tf_op jit(solution)/shard_map/reduce_scatter | solution.py:79
  414.0 1.1 copy-start.81
  (43 other events, 43.3 us)
Sparse Core Ops, SparseCore 0:
  412.6 6.7 reduce-scatter.2
  423.8 13.6 reduce-scatter.4
